TPU v7x, 32 devices: a whole 2x2x4 slice. The times are simulated.
32 devices in a mesh: grp: 1, row: 32 (over z, y, x, core), col: 1.
Axes of the slice: x: 2, y: 2, z: 4, core: 2. Of those that a mesh axis runs over, the one named last changes fastest.
Arguments:
- pair_map: bfloat16 [128, 128, 288], P(('grp', 'row'), 'col'), may hold values from -6 to 6
- norm_in: float32 [288], replicated, may hold values from 0.1 to 1.9
- w_query: bfloat16 [288, 256], replicated, may hold values from -12 to 12
- w_key: bfloat16 [288, 256], replicated, may hold values from -1 to 1
- w_value: bfloat16 [288, 256], replicated, may hold values from -0.375 to 0.375
- w_gate: bfloat16 [288, 256], replicated, may hold values from -0.375 to 0.375
- w_out: bfloat16 [256, 288], replicated, may hold values from -3 to 3
- norm_mid: float32 [288], replicated, may hold values from 0.1 to 1.9
- norm_out: float32 [288], replicated, may hold values from 0.1 to 1.9
- w_up: bfloat16 [288, 1152], replicated, may hold values from -0.375 to 0.375
- w_down: bfloat16 [1152, 288], replicated, may hold values from -0.1875 to 0.1875
Outputs:
- updated: bfloat16 [128, 128, 288], P(('grp', 'row'), 'col')
All inputs are finite; a program needn't handle non-finite values.
Results may differ from a plain program's by a relative error of at most 0.014.
Values may be sent and summed in bfloat16 or wider, within the bound.
A program may use at most 64 MiB of HBM per device.

v0:
```python
import jax
import jax.numpy as jnp
from jax import lax
from jax.sharding import PartitionSpec as P

HEADS = 8
HEAD_DIM = 32


epsilon = 1e-06


def normalize(inputs, gain):
    mean_square = jnp.mean(inputs * inputs, axis=-1, keepdims=True)
    return inputs * lax.rsqrt(mean_square + epsilon) * gain


def attend_rows(pair_rows, norm_in, w_query, w_key, w_value, w_gate, w_out, norm_mid):
    row_count = pair_rows.shape[0]
    length = pair_rows.shape[1]
    channels = pair_rows.shape[2]
    widened = pair_rows.astype(jnp.float32)
    normed = normalize(widened, norm_in).astype(jnp.bfloat16).reshape(row_count * length, channels)

    def project(weight):
        return jnp.dot(normed, weight, preferred_element_type=jnp.float32).astype(jnp.bfloat16)

    query_rows = project(w_query).reshape(row_count, length, HEADS, HEAD_DIM).transpose(2, 0, 1, 3)
    key_rows = project(w_key).reshape(row_count, length, HEADS, HEAD_DIM).transpose(2, 0, 1, 3)
    value_rows = project(w_value).reshape(row_count, length, HEADS, HEAD_DIM).transpose(2, 0, 1, 3)
    gate_rows = project(w_gate)
    score_scale = HEAD_DIM ** (-0.5)

    def one_head(triple):
        query_head, key_head, value_head = triple
        scores = (
            jnp.einsum("mqd,mkd->mqk", query_head, key_head, preferred_element_type=jnp.float32)
            * score_scale
        )
        scores = scores - jnp.max(scores, axis=-1, keepdims=True)
        expanded = jnp.exp(scores)
        probabilities = (expanded / jnp.sum(expanded, axis=-1, keepdims=True)).astype(jnp.bfloat16)
        return jnp.einsum(
            "mqk,mkd->mqd", probabilities, value_head, preferred_element_type=jnp.float32
        )

    head_outputs = lax.map(one_head, (query_rows, key_rows, value_rows))
    merged = head_outputs.transpose(1, 2, 0, 3).reshape(row_count * length, HEADS * HEAD_DIM)
    gated = (merged * jax.nn.sigmoid(gate_rows.astype(jnp.float32))).astype(jnp.bfloat16)
    update = jnp.dot(gated, w_out, preferred_element_type=jnp.float32).reshape(
        row_count, length, channels
    )
    return normalize(widened + update, norm_mid).astype(jnp.bfloat16)


def feed_forward(sym_rows, norm_out, w_up, w_down):
    shape_in = sym_rows.shape
    flat = sym_rows.reshape(-1, shape_in[-1]).astype(jnp.float32)
    normed = normalize(flat, norm_out).astype(jnp.bfloat16)
    hidden = jnp.maximum(jnp.dot(normed, w_up, preferred_element_type=jnp.float32), 0.0).astype(
        jnp.bfloat16
    )
    result = flat + jnp.dot(hidden, w_down, preferred_element_type=jnp.float32)
    return result.astype(jnp.bfloat16).reshape(shape_in)


def local(
    pair_map, norm_in, w_query, w_key, w_value, w_gate, w_out, norm_mid, norm_out, w_up, w_down
):
    col_count = lax.axis_size("col")
    row_count = lax.axis_size("row")
    tile_rows = pair_map.shape[0]
    tile_cols = pair_map.shape[1]
    channels = pair_map.shape[2]
    own_rows = tile_rows // col_count
    halves = pair_map.reshape(col_count, own_rows, tile_cols, channels)
    attended = attend_rows(
        lax.all_to_all(halves, "col", split_axis=0, concat_axis=2, tiled=True)[0],
        norm_in,
        w_query,
        w_key,
        w_value,
        w_gate,
        w_out,
        norm_mid,
    )[None][0]
    length = attended.shape[1]
    ordered = attended.reshape(own_rows, row_count, col_count, own_rows, channels).transpose(
        3, 1, 2, 0, 4
    )
    partial_move = lax.all_to_all(ordered, "col", split_axis=2, concat_axis=2, tiled=True)
    arrived = lax.all_to_all(partial_move, "row", split_axis=1, concat_axis=1, tiled=True)
    mirrored = arrived.reshape(own_rows, length, channels)
    symmetric = ((attended.astype(jnp.float32) + mirrored.astype(jnp.float32)) * 0.5).astype(
        jnp.bfloat16
    )
    finished = feed_forward(symmetric, norm_out, w_up, w_down).reshape(
        own_rows, col_count, tile_cols, channels
    )
    returned = lax.all_to_all(finished, "col", split_axis=1, concat_axis=0, tiled=True)
    return returned.reshape(tile_rows, tile_cols, channels)


def solution(mesh):
    placed = (P(("grp", "row"), "col", None), P(), P(), P(), P(), P(), P(), P(), P(), P(), P())
    return jax.shard_map(
        local, mesh=mesh, in_specs=placed, out_specs=P(("grp", "row"), "col", None), check_vma=False
    )
```

profile of v0, /device:TPU:0, one launch (start us, length us, event | category | flops | bytes accessed | tf_op | source)
XLA Modules:
  0.0 39.7 jit_solution(12040283022141453792)
XLA Ops:
  0.0 1.1 %fusion.21 = f32[4,128]{1,0:T(4,128)S(1)} fusion(bf16[4,128,288]{1,2,0:T(8,128)(2,1)} %param.13), kind=kLoop, calls=%fused_computation.41 | loop fusion | flops 441856 | bytes 296960 | tf_op jit(solution)/shard_map/reduce_sum | solution.py:14
  1.1 1.4 %convolution_convert_fusion.3 = bf16[512,256]{1,0:T(8,128)(2,1)S(1)} fusion(bf16[288,256]{1,0:T(8,128)(2,1)} %param.15, bf16[4,128,288]{1,2,0:T(8,128)(2,1)} %param.13, f32[288]{0:T(512)} %param.14, f32[4,128]{1,0:T(4,128)S(1)} %add_rsqrt_fusion.1), kind=kOutput, calls=%fused_computation.32 | convolution fusion | flops 76218368 | bytes 707712 | tf_op jit(solution)/shard_map/dot_general | solution.py:26
  2.8 0.7 %copy-done.1 = bf16[4,128,288]{1,2,0:T(8,128)(2,1)S(1)} copy-done((bf16[4,128,288]{1,2,0:T(8,128)(2,1)S(1)}, bf16[4,128,288]{1,2,0:T(8,128)(2,1)}, u32[]{:S(2)}) %copy-start.1) | copy-done | bytes 294936
  3.6 0.4 %convolution_convert_fusion.2 = bf16[512,256]{1,0:T(8,128)(2,1)S(1)} fusion(bf16[288,256]{1,0:T(8,128)(2,1)S(1)} %copy-done.4, bf16[4,128,288]{1,2,0:T(8,128)(2,1)S(1)} %copy-done.1, f32[288]{0:T(512)S(1)} %copy-done.8, f32[4,128]{1,0:T(4,128)S(1)} %add_rsqrt_fusion.1), kind=kOutput, calls=%fused_computation.31 | convolution fusion | flops 76218368 | bytes 707712 | tf_op jit(solution)/shard_map/dot_general | solution.py:26
  4.2 0.7 %copy-done.5 = bf16[288,256]{1,0:T(8,128)(2,1)S(1)} copy-done((bf16[288,256]{1,0:T(8,128)(2,1)S(1)}, bf16[288,256]{1,0:T(8,128)(2,1)}, u32[]{:S(2)}) %copy-start.5) | copy-done | bytes 147480
  4.9 0.4 %convolution_convert_fusion.1 = bf16[512,256]{1,0:T(8,128)(2,1)S(1)} fusion(bf16[288,256]{1,0:T(8,128)(2,1)S(1)} %copy-done.5, bf16[4,128,288]{1,2,0:T(8,128)(2,1)S(1)} %copy-done.1, f32[288]{0:T(512)S(1)} %copy-done.8, f32[4,128]{1,0:T(4,128)S(1)} %add_rsqrt_fusion.1), kind=kOutput, calls=%fused_computation.30 | convolution fusion | flops 76218368 | bytes 707712 | tf_op jit(solution)/shard_map/dot_general | solution.py:26
  5.5 6.4 %while.10 = (s32[]{:T(128)}, f32[8,4,128,32]{2,3,1,0:T(8,128)S(1)}, bf16[8,4,128,32]{2,1,3,0:T(4,128)(2,1)S(1)}, bf16[8,4,128,32]{2,1,3,0:T(4,128)(2,1)S(1)}, bf16[8,4,128,32]{2,1,3,0:T(4,128)(2,1)S(1)}, /*index=5*/s32[]{:T(128)}) while((s32[]{:T(128)}, f32[8,4,128,32]{2,3,1,0:T(8,128)S(1)}, bf16[8,4,128,32]{2,1,3,0:T(4,128)(2,1)S(1)}, ...), condition=%wide.region_4.5_spmd, body=%wide.region_1.4_spmd.sunk | while | flops 13042432 | bytes 1216593 | solution.py:47
  5.8 0.3 fusion.70
  6.6 0.3 fusion.70
  7.4 0.3 fusion.70
  8.3 0.3 fusion.70
  9.1 0.3 fusion.70
  9.9 0.3 fusion.70
  10.7 0.3 fusion.70
  11.5 0.3 fusion.70
  12.0 0.3 copy.100
  12.6 0.7 %copy-done.6 = bf16[256,288]{0,1:T(8,128)(2,1)S(1)} copy-done((bf16[256,288]{0,1:T(8,128)(2,1)S(1)}, bf16[256,288]{0,1:T(8,128)(2,1)}, u32[]{:S(2)}) %copy-start.6) | copy-done | bytes 147480
  13.3 0.8 %convolution_bitcast_fusion.1 = f32[36,4,8,128]{3,2,1,0:T(8,128)S(1)} fusion(bf16[256,288]{0,1:T(8,128)(2,1)S(1)} %copy-done.6, f32[512,256]{1,0:T(8,128)S(1)} %copy.101, bf16[288,256]{1,0:T(8,128)(2,1)S(1)} %copy-done.7, bf16[4,128,288]{1,2,0:T(8,128)(2,1)S(1)} %copy-done.1, f32[288]{0:T(512)S(1)} %copy-done.8, f32[4,128]{1,0:T(4,128)S(1)} %add_rsqrt_fusion.1), kind=kOutput, calls=%fused_computation.20 | convolution fusion | flops 152502272 | bytes 1707136 | tf_op jit(solution)/shard_map/dot_general | solution.py:50
  14.3 0.6 %copy-done.2 = f32[288]{0:T(512)S(1)} copy-done((f32[288]{0:T(512)S(1)}, f32[288]{0:T(512)}, u32[]{:S(2)}) %copy-start.2) | copy-done | bytes 1176
  15.2 20.4 %all_to_all.5 = bf16[4,32,1,4,288]{4,3,0,2,1:T(4,128)(2,1)S(1)} all-to-all(bf16[4,32,1,4,288]{4,3,0,2,1:T(4,128)(2,1)S(1)} %bitcast.116), channel_id=1, replica_groups=mesh['grp'=1,'row'=32,'col'=1] {'row'}, dimensions={1} | all-to-all | bytes 589824 | tf_op jit(solution)/shard_map/all_to_all | solution.py:92
  35.7 0.5 %copy.108 = f32[4,32,1,4,288]{4,0,3,1,2:T(4,128)S(1)} copy(f32[4,32,1,4,288]{4,1,3,2,0:T(8,128)S(1)} %copy_convert_fusion) | data formatting | bytes 1179648 | tf_op jit(solution)/shard_map/convert_element_type | solution.py:94
  36.7 0.9 %copy-done.3 = bf16[288,1152]{1,0:T(8,128)(2,1)S(1)} copy-done((bf16[288,1152]{1,0:T(8,128)(2,1)S(1)}, bf16[288,1152]{1,0:T(8,128)(2,1)}, u32[]{:S(2)}) %copy-start.3) | copy-done | bytes 663576
  37.6 1.3 %fusion.19 = bf16[36,4,8,128]{3,2,1,0:T(8,128)(2,1)S(1)} fusion(bf16[1152,288]{0,1:T(8,128)(2,1)S(1)} %copy-done, bf16[288,1152]{1,0:T(8,128)(2,1)S(1)} %copy-done.3, f32[4,36,8,128]{3,2,1,0:T(8,128)S(1)} %get-tuple-element.71, f32[288]{0:T(512)S(1)} %copy-done.9, f32[512]{0:T(512)S(1)} %rsqrt_bitcast_fusion), kind=kOutput, calls=%fused_computation.34 | convolution fusion | flops 681394176 | bytes 2215040 | tf_op jit(solution)/shard_map/dot_general | solution.py:63
  39.0 0.8 %copy.171 = bf16[36,4,8,128]{3,2,0,1:T(8,128)(2,1)} copy(bf16[36,4,8,128]{3,2,1,0:T(8,128)(2,1)S(1)} %fusion.19) | data formatting | bytes 589824 | tf_op jit(solution)/shard_map/reshape;reshape;reshape | solution.py:101
  (65 shorter events, 5.8 us)
Async XLA Ops:
  0.0 36.7 %copy-start = (bf16[1152,288]{0,1:T(8,128)(2,1)S(1)}, bf16[1152,288]{0,1:T(8,128)(2,1)}, u32[]{:S(2)}) copy-start(bf16[1152,288]{0,1:T(8,128)(2,1)} %param.23) | copy-start | bytes 1990660
  2.6 1.0 %copy-start.1 = (bf16[4,128,288]{1,2,0:T(8,128)(2,1)S(1)}, bf16[4,128,288]{1,2,0:T(8,128)(2,1)}, u32[]{:S(2)}) copy-start(bf16[4,128,288]{1,2,0:T(8,128)(2,1)} %param.13) | copy-start | bytes 884740
  2.6 1.0 %copy-start.4 = (bf16[288,256]{1,0:T(8,128)(2,1)S(1)}, bf16[288,256]{1,0:T(8,128)(2,1)}, u32[]{:S(2)}) copy-start(bf16[288,256]{1,0:T(8,128)(2,1)} %param.16) | copy-start | bytes 442372
  2.6 1.0 %copy-start.8 = (f32[288]{0:T(512)S(1)}, f32[288]{0:T(512)}, u32[]{:S(2)}) copy-start(f32[288]{0:T(512)} %param.14) | copy-start | bytes 3460
  4.0 0.9 %copy-start.5 = (bf16[288,256]{1,0:T(8,128)(2,1)S(1)}, bf16[288,256]{1,0:T(8,128)(2,1)}, u32[]{:S(2)}) copy-start(bf16[288,256]{1,0:T(8,128)(2,1)} %param.17) | copy-start | bytes 442372
  12.4 0.9 %copy-start.6 = (bf16[256,288]{0,1:T(8,128)(2,1)S(1)}, bf16[256,288]{0,1:T(8,128)(2,1)}, u32[]{:S(2)}) copy-start(bf16[256,288]{0,1:T(8,128)(2,1)} %param.19) | copy-start | bytes 442372
  12.4 1.0 %copy-start.7 = (bf16[288,256]{1,0:T(8,128)(2,1)S(1)}, bf16[288,256]{1,0:T(8,128)(2,1)}, u32[]{:S(2)}) copy-start(bf16[288,256]{1,0:T(8,128)(2,1)} %param.18) | copy-start | bytes 442372
  14.2 0.7 %copy-start.2 = (f32[288]{0:T(512)S(1)}, f32[288]{0:T(512)}, u32[]{:S(2)}) copy-start(f32[288]{0:T(512)} %param.20) | copy-start | bytes 3460
  36.5 1.1 %copy-start.3 = (bf16[288,1152]{1,0:T(8,128)(2,1)S(1)}, bf16[288,1152]{1,0:T(8,128)(2,1)}, u32[]{:S(2)}) copy-start(bf16[288,1152]{1,0:T(8,128)(2,1)} %param.22) | copy-start | bytes 1990660
  36.5 1.1 %copy-start.9 = (f32[288]{0:T(512)S(1)}, f32[288]{0:T(512)}, u32[]{:S(2)}) copy-start(f32[288]{0:T(512)} %param.21) | copy-start | bytes 3460
where the time goes:
time: 40 us; the launch traced here: 39.7 us
  blocking collectives  20.4 us (51%)
  matrix products  10.2 us (25%)
  local copies, waits for them, and re-layouts  7.17 us (18%)
  other arithmetic  1.55 us (4%)
    all_to_all x1, blocking collectives, local(): lax.all_to_all(partial_move, 'row', split_axis=1, concat_axis=1, tiled=True)  20.4 us
    unnamed x21, local copies, waits for them, and re-layouts  3.77 us
    sub x8, matrix products, one_head(): scores = scores - jnp.max(scores, axis=-1, keepdims=True)  2.4 us
    dot_general x3, matrix products, project(): jnp.dot(normed, weight, preferred_element_type=jnp.float32)  2.25 us
    dot_general x8, matrix products, one_head(): jnp.einsum('mqd,mkd->mqk', query_head, key_head, preferred_element_type=j...  1.87 us
    dot_general x8, matrix products, one_head(): jnp.einsum('mqk,mkd->mqd', probabilities, value_head, preferred_element_t...  1.52 us
    dot_general x1, matrix products, feed_forward(): result = flat + jnp.dot(hidden, w_down, preferred_element_type=jnp.float32)  1.33 us
    reduce_sum x3, other arithmetic, normalize(): mean_square = jnp.mean(inputs * inputs, axis=-1, keepdims=True)  1.31 us

commit v1 on v0

v1 whole, which is shorter than its diff:
```python
import functools

import jax
import jax.numpy as jnp
from jax import lax
from jax.experimental import pallas as pl
from jax.experimental.pallas import tpu as pltpu
from jax.sharding import PartitionSpec as P

HEADS = 8
HEAD_DIM = 32


epsilon = 1e-06


def normalize(inputs, gain):
    mean_square = jnp.mean(inputs * inputs, axis=-1, keepdims=True)
    return inputs * lax.rsqrt(mean_square + epsilon) * gain


def contract(left, right, left_dim, right_dim):
    return lax.dot_general(
        left, right, (((left_dim,), (right_dim,)), ((), ())), preferred_element_type=jnp.float32
    )


def exchange_matrix(pairs, own_rows, length, outgoing):
    target = lax.broadcasted_iota(jnp.int32, (pairs, pairs), 0)
    source = lax.broadcasted_iota(jnp.int32, (pairs, pairs), 1)
    block = own_rows * own_rows
    if outgoing:
        device = target // block
        column = (target % block) // own_rows
        row = target % own_rows
        wanted = row * length + device * own_rows + column
    else:
        column = target // length
        device = (target % length) // own_rows
        row = target % own_rows
        wanted = device * block + column * own_rows + row
    return jnp.where(source == wanted, 1.0, 0.0).astype(jnp.bfloat16)


def attend_kernel(
    x_ref, norm_in, w_query, w_key, w_value, w_gate, w_out, norm_mid, own_ref, send_ref, merged_ref
):
    own_rows, length, channels = x_ref.shape
    pairs = own_rows * length
    widened = x_ref[...].reshape(pairs, channels).astype(jnp.float32)
    normed = normalize(widened, norm_in[...]).astype(jnp.bfloat16)
    queries = contract(w_query[...], normed, 0, 1).astype(jnp.bfloat16)
    keys = contract(w_key[...], normed, 0, 1).astype(jnp.bfloat16)
    values = contract(w_value[...], normed, 0, 1).astype(jnp.bfloat16)
    gates = jax.nn.sigmoid(contract(w_gate[...], normed, 0, 1))
    scale = HEAD_DIM ** (-0.5)
    for row in range(own_rows):
        span = slice(row * length, (row + 1) * length)
        for head in range(HEADS):
            part = slice(head * HEAD_DIM, (head + 1) * HEAD_DIM)
            scores = contract(keys[part, span], queries[part, span], 0, 0)
            expanded = jnp.exp((scores - jnp.max(scores, axis=0, keepdims=True)) * scale)
            total = jnp.sum(expanded, axis=0, keepdims=True)
            attended = contract(values[part, span], expanded.astype(jnp.bfloat16), 1, 0)
            merged_ref[part, span] = (attended * (1.0 / total) * gates[part, span]).astype(
                jnp.bfloat16
            )
    update = contract(merged_ref[...], w_out[...], 0, 0)
    rowwise = normalize(widened + update, norm_mid[...]).astype(jnp.bfloat16)
    own_ref[...] = rowwise
    send_ref[...] = contract(
        exchange_matrix(pairs, own_rows, length, True), rowwise, 1, 0
    ).astype(jnp.bfloat16)


def transition_kernel(own_rows, length, own_ref, arrived_ref, norm_out, w_up, w_down, out_ref):
    pairs = own_rows * length
    mirrored = contract(exchange_matrix(pairs, own_rows, length, False), arrived_ref[...], 1, 0)
    symmetric = ((own_ref[...].astype(jnp.float32) + mirrored) * 0.5).astype(jnp.bfloat16)
    flat = symmetric.astype(jnp.float32)
    normed = normalize(flat, norm_out[...]).astype(jnp.bfloat16)
    hidden = jnp.maximum(contract(normed, w_up[...], 1, 0), 0.0).astype(jnp.bfloat16)
    out_ref[...] = (flat + contract(hidden, w_down[...], 1, 0)).astype(jnp.bfloat16)


def local(
    pair_map, norm_in, w_query, w_key, w_value, w_gate, w_out, norm_mid, norm_out, w_up, w_down
):
    col_count = lax.axis_size("col")
    row_count = lax.axis_size("row")
    tile_rows, tile_cols, channels = pair_map.shape
    own_rows = tile_rows // col_count
    length = tile_cols * col_count
    pairs = own_rows * length
    hidden = w_query.shape[1]
    rows = pair_map
    if col_count > 1:
        halves = pair_map.reshape(col_count, own_rows, tile_cols, channels)
        rows = lax.all_to_all(halves, "col", split_axis=0, concat_axis=2, tiled=True)[0]
    whole = pl.BlockSpec(memory_space=pltpu.VMEM)
    own, send = pl.pallas_call(
        attend_kernel,
        out_shape=[jax.ShapeDtypeStruct((pairs, channels), jnp.bfloat16)] * 2,
        in_specs=[whole] * 8,
        out_specs=[whole] * 2,
        scratch_shapes=[pltpu.VMEM((hidden, pairs), jnp.bfloat16)],
    )(rows, norm_in[None], w_query, w_key, w_value, w_gate, w_out, norm_mid[None])
    axes = ("row", "col") if col_count > 1 else "row"
    arrived = lax.all_to_all(
        send.reshape(row_count * col_count, own_rows * own_rows, channels),
        axes,
        split_axis=0,
        concat_axis=0,
        tiled=True,
    ).reshape(pairs, channels)
    finished = pl.pallas_call(
        functools.partial(transition_kernel, own_rows, length),
        out_shape=jax.ShapeDtypeStruct((pairs, channels), jnp.bfloat16),
        in_specs=[whole] * 5,
        out_specs=whole,
    )(own, arrived, norm_out[None], w_up, w_down)
    if col_count == 1:
        return finished.reshape(tile_rows, tile_cols, channels)
    returned = lax.all_to_all(
        finished.reshape(own_rows, col_count, tile_cols, channels),
        "col",
        split_axis=1,
        concat_axis=0,
        tiled=True,
    )
    return returned.reshape(tile_rows, tile_cols, channels)


def solution(mesh):
    placed = (P(("grp", "row"), "col", None), P(), P(), P(), P(), P(), P(), P(), P(), P(), P())
    return jax.shard_map(
        local, mesh=mesh, in_specs=placed, out_specs=P(("grp", "row"), "col", None), check_vma=False
    )
```

time: 40 us -> 41.4 us (1.035)
  blocking collectives: 20.4 us -> 0 us
  Pallas kernels: 0 us -> 13.3 us
  waiting for transfers between devices: 0 us -> 11.4 us
  matrix products: 10.2 us -> 0 us
  starting transfers between devices: 0 us -> 7.32 us
  local copies, waits for them, and re-layouts: 7.17 us -> 9.02 us
  other arithmetic: 1.55 us -> 0 us
    all_to_all x1 -> x0, blocking collectives: 20.4 us -> none  [local(): lax.all_to_all(partial_move, 'row', split_axis=1, concat_axis=1, tiled=True)]
    pallas_call x0 -> x2, Pallas kernels: none -> 13.3 us  [the longest x1 9.01 us: local(): pl.pallas_call(attend_kernel, out_shape=[jax.ShapeDtypeStruct((pairs, cha...]
    all_to_all x0 -> x1, waiting for transfers between devices: none -> 11.4 us  [local(): lax.all_to_all(send.reshape(row_count * col_count, own_rows * own_rows, c...]
    dot_general x21 -> x0, matrix products: 7.77 us -> none  [the longest x3 2.25 us: project(): jnp.dot(normed, weight, preferred_element_type=jnp.float32)]
    all_to_all x0 -> x1, starting transfers between devices: none -> 7.32 us  [local(): lax.all_to_all(send.reshape(row_count * col_count, own_rows * own_rows, c...]
    broadcast_in_dim x0 -> x3, local copies, waits for them, and re-layouts: none -> 2.47 us  [the longest x1 1.32 us: local(): norm_in[None]]
    sub x8 -> x0, matrix products: 2.4 us -> none  [one_head(): scores = scores - jnp.max(scores, axis=-1, keepdims=True)]
    reshape x4 -> x1, local copies, waits for them, and re-layouts: 0.39 us -> 1.88 us  [local(): return finished.reshape(tile_rows, tile_cols, channels)]
  transfers between devices with their start and end apart: 0 -> 1, of which waited for: 0 -> 1; matrix products, arithmetic and copies ran while one was open for 0% -> 4% of each run, Pallas kernels for 0% -> 0%
where the time goes in v1:
time: 41.4 us; the launch traced here: 41.1 us
  Pallas kernels  13.3 us (32%)
  waiting for transfers between devices  11.4 us (28%)
  local copies, waits for them, and re-layouts  9.02 us (22%)
  starting transfers between devices  7.32 us (18%)
    all_to_all x1, waiting for transfers between devices, local(): lax.all_to_all(send.reshape(row_count * col_count, own_rows * own_rows, c...  11.4 us
    pallas_call x1, Pallas kernels, local(): pl.pallas_call(attend_kernel, out_shape=[jax.ShapeDtypeStruct((pairs, cha...  9.01 us
    all_to_all x1, starting transfers between devices, local(): lax.all_to_all(send.reshape(row_count * col_count, own_rows * own_rows, c...  7.32 us
    unnamed x13, local copies, waits for them, and re-layouts  4.67 us
    pallas_call x1, Pallas kernels, local(): pl.pallas_call(functools.partial(transition_kernel, own_rows, length), ou...  4.27 us
    reshape x1, local copies, waits for them, and re-layouts, local(): return finished.reshape(tile_rows, tile_cols, channels)  1.88 us
    broadcast_in_dim x1, local copies, waits for them, and re-layouts, local(): norm_in[None]  1.32 us
  transfers between devices with their start and end apart: 1, of which 1 were waited for; matrix products, arithmetic and copies ran while one was open for 4% of the time, Pallas kernels for 0%

profile of v1, /device:TPU:0, one launch (start us, length us, event | category | flops | bytes accessed | tf_op | source)
XLA Modules:
  0.0 41.1 jit_solution(9338487345370693650)
XLA Ops:
  0.0 0.0 copy-start.3
  0.0 0.0 copy-start.2
  0.0 1.3 %broadcast_in_dim.9.norm_in = f32[1,288]{1,0:T(1,128)} reshape(f32[288]{0:T(512)} %param.12) | data formatting | bytes 2304 | tf_op jit(solution)/shard_map/broadcast_in_dim | solution.py:107
  1.3 0.0 copy-done.3
  1.3 0.6 %broadcast_in_dim.10.norm_mid = f32[1,288]{1,0:T(1,128)} reshape(f32[288]{0:T(512)S(1)} %copy-done.3) | data formatting | bytes 2304 | tf_op jit(solution)/shard_map/broadcast_in_dim | solution.py:107
  1.9 1.7 %copy.13.w_out = bf16[256,288]{1,0:T(8,128)(2,1)} copy(bf16[256,288]{0,1:T(8,128)(2,1)} %param.17) | data formatting | bytes 294912 | tf_op args[6]
  3.6 0.0 copy-done.2
  3.6 0.9 %copy.12.x_ref = bf16[4,128,288]{2,1,0:T(8,128)(2,1)} copy(bf16[4,128,288]{1,2,0:T(8,128)(2,1)S(1)} %copy-done.2) | data formatting | bytes 589824 | tf_op args[0]
  4.6 9.0 %shard_map.109 = (bf16[512,288]{1,0:T(8,128)(2,1)}, bf16[512,288]{1,0:T(8,128)(2,1)}) custom-call(bf16[4,128,288]{2,1,0:T(8,128)(2,1)} %copy.12.x_ref, f32[1,288]{1,0:T(1,128)} %broadcast_in_dim.9.norm_in, bf16[288,256]{1,0:T(8,128)(2,1)} %w_query.1, bf16[288,256]{1,0:T(8,128)(2,1)} %w_key.1, bf16[288,256]{1,0:T(8,128)(2,1)} %w_value.1, ...), custom_call_target="tpu_custom_call" | custom-call | tf_op jit(solution)/shard_map/pallas_call | solution.py:101
  13.6 0.0 copy-start.1
  13.6 0.0 copy-start.4
  13.6 7.3 %all-to-all-start = ((bf16[32,16,288]{2,1,0:T(8,128)(2,1)}), bf16[32,16,288]{2,1,0:T(8,128)(2,1)S(1)}, u32[]{:S(2)}, u32[]{:S(2)}) async-start(bf16[32,16,288]{2,1,0:T(8,128)(2,1)} %bitcast.5), calls=%async_computation | async-start | bytes 786432 | tf_op jit(solution)/shard_map/all_to_all | solution.py:109
  20.9 0.0 copy-done.4
  20.9 0.6 %broadcast_in_dim.11.norm_out = f32[1,288]{1,0:T(1,128)} reshape(f32[288]{0:T(512)S(1)} %copy-done.4) | data formatting | bytes 2304 | tf_op jit(solution)/shard_map/broadcast_in_dim | solution.py:121
  21.5 0.0 copy-done.1
  21.5 1.2 %copy.14.w_down = bf16[1152,288]{1,0:T(8,128)(2,1)} copy(bf16[1152,288]{0,1:T(8,128)(2,1)S(1)} %copy-done.1) | data formatting | bytes 1327104 | tf_op args[10]
  22.7 11.4 %all-to-all-done = bf16[32,16,288]{2,1,0:T(8,128)(2,1)S(1)} async-done(((bf16[32,16,288]{2,1,0:T(8,128)(2,1)}), bf16[32,16,288]{2,1,0:T(8,128)(2,1)S(1)}, u32[]{:S(2)}, u32[]{:S(2)}) %all-to-all-start) | async-done | bytes 294944 | tf_op jit(solution)/shard_map/all_to_all | solution.py:109
  34.2 0.0 copy-start
  34.2 0.8 %copy-done = bf16[32,16,288]{2,1,0:T(8,128)(2,1)} copy-done((bf16[32,16,288]{2,1,0:T(8,128)(2,1)}, bf16[32,16,288]{2,1,0:T(8,128)(2,1)S(1)}, u32[]{:S(2)}) %copy-start) | copy-done | bytes 294936
  34.9 4.3 %shard_map.110 = bf16[512,288]{1,0:T(8,128)(2,1)} custom-call(bf16[512,288]{1,0:T(8,128)(2,1)} %get-tuple-element.7.own_ref, bf16[512,288]{1,0:T(8,128)(2,1)} %bitcast.3, f32[1,288]{1,0:T(1,128)} %broadcast_in_dim.11.norm_out, bf16[288,1152]{1,0:T(8,128)(2,1)} %w_up.1, bf16[1152,288]{1,0:T(8,128)(2,1)} %copy.14.w_down), custom_call_target="tpu_custom_call" | custom-call | tf_op jit(solution)/shard_map/pallas_call | solution.py:116
  39.2 1.9 %copy.15 = bf16[4,128,288]{1,2,0:T(8,128)(2,1)} copy(bf16[4,128,288]{2,1,0:T(8,128)(2,1)} %bitcast.4) | data formatting | bytes 589824 | tf_op jit(solution)/shard_map/reshape | solution.py:123
Async XLA Ops:
  0.0 1.3 %copy-start.3 = (f32[288]{0:T(512)S(1)}, f32[288]{0:T(512)}, u32[]{:S(2)}) copy-start(f32[288]{0:T(512)} %param.18) | copy-start | bytes 3460
  0.0 3.6 %copy-start.2 = (bf16[4,128,288]{1,2,0:T(8,128)(2,1)S(1)}, bf16[4,128,288]{1,2,0:T(8,128)(2,1)}, u32[]{:S(2)}) copy-start(bf16[4,128,288]{1,2,0:T(8,128)(2,1)} %param.11) | copy-start | bytes 884740
  13.6 7.9 %copy-start.1 = (bf16[1152,288]{0,1:T(8,128)(2,1)S(1)}, bf16[1152,288]{0,1:T(8,128)(2,1)}, u32[]{:S(2)}) copy-start(bf16[1152,288]{0,1:T(8,128)(2,1)} %param.21) | copy-start | bytes 1990660
  13.6 7.3 %copy-start.4 = (f32[288]{0:T(512)S(1)}, f32[288]{0:T(512)}, u32[]{:S(2)}) copy-start(f32[288]{0:T(512)} %param.19) | copy-start | bytes 3460
  13.6 20.6 %all-to-all-start = ((bf16[32,16,288]{2,1,0:T(8,128)(2,1)}), bf16[32,16,288]{2,1,0:T(8,128)(2,1)S(1)}, u32[]{:S(2)}, u32[]{:S(2)}) async-start(bf16[32,16,288]{2,1,0:T(8,128)(2,1)} %bitcast.5), calls=%async_computation | async-start | bytes 786432 | tf_op jit(solution)/shard_map/all_to_all | solution.py:109
  34.2 0.8 %copy-start = (bf16[32,16,288]{2,1,0:T(8,128)(2,1)}, bf16[32,16,288]{2,1,0:T(8,128)(2,1)S(1)}, u32[]{:S(2)}) copy-start(bf16[32,16,288]{2,1,0:T(8,128)(2,1)S(1)} %all-to-all-done) | copy-start | bytes 884740

commit v2 on v1

v2 whole, which is shorter than its diff:
```python
import functools

import jax
import jax.numpy as jnp
from jax import lax
from jax.experimental import pallas as pl
from jax.experimental.pallas import tpu as pltpu
from jax.sharding import PartitionSpec as P

HEADS = 8
HEAD_DIM = 32
LANES = 128


epsilon = 1e-06


def normalize(inputs, gain):
    mean_square = jnp.mean(inputs * inputs, axis=0, keepdims=True)
    return inputs * lax.rsqrt(mean_square + epsilon) * gain


def contract(left, right, left_dim, right_dim):
    return lax.dot_general(
        left, right, (((left_dim,), (right_dim,)), ((), ())), preferred_element_type=jnp.float32
    )


def upright(gain, pairs):
    column = jnp.broadcast_to(gain, (LANES, gain.shape[1])).T
    return jnp.concatenate([column] * (pairs // LANES), axis=1)


def flatten(ref):
    return jnp.concatenate([ref[row] for row in range(ref.shape[0])], axis=1)


def outgoing(slots, padded, own_rows, length):
    shape = (slots, own_rows * length)
    slot = lax.broadcasted_iota(jnp.int32, shape, 0)
    pair = lax.broadcasted_iota(jnp.int32, shape, 1)
    within = slot % padded
    wanted = (within % own_rows) * length + (slot // padded) * own_rows + within // own_rows
    wanted = jnp.where(within < own_rows * own_rows, wanted, -1)
    return jnp.where(pair == wanted, 1.0, 0.0).astype(jnp.bfloat16)


def incoming(slots, padded, own_rows, length):
    shape = (slots, own_rows * length)
    slot = lax.broadcasted_iota(jnp.int32, shape, 0)
    pair = lax.broadcasted_iota(jnp.int32, shape, 1)
    device = (pair % length) // own_rows
    wanted = device * padded + (pair // length) * own_rows + pair % own_rows
    return jnp.where(slot == wanted, 1.0, 0.0).astype(jnp.bfloat16)


def attend_kernel(
    count,
    cols,
    x_ref,
    norm_in,
    w_query,
    w_key,
    w_value,
    w_gate,
    w_out,
    norm_mid,
    sym_ref,
    merged_ref,
    send_ref,
    land_ref,
    send_sem,
    recv_sem,
):
    own_rows, channels, length = x_ref.shape
    pairs = own_rows * length
    padded = send_ref.shape[1]
    me = lax.axis_index("row") * cols + lax.axis_index("col")

    def place(offset):
        other = lax.rem(me + offset, count)
        return {"row": other // cols, "col": lax.rem(other, cols)}

    def transfer(offset):
        other = lax.rem(me + offset, count)
        return pltpu.make_async_remote_copy(
            src_ref=send_ref.at[other],
            dst_ref=land_ref.at[me],
            send_sem=send_sem.at[offset],
            recv_sem=recv_sem.at[offset],
            device_id=place(offset),
            device_id_type=pl.DeviceIdType.MESH,
        )

    barrier = pltpu.get_barrier_semaphore()

    @pl.loop(1, count)
    def _(offset):
        pl.semaphore_signal(
            barrier, inc=1, device_id=place(offset), device_id_type=pl.DeviceIdType.MESH
        )

    widened = flatten(x_ref).astype(jnp.float32)
    normed = normalize(widened, upright(norm_in[...], pairs)).astype(jnp.bfloat16)
    queries = contract(w_query[...], normed, 0, 0).astype(jnp.bfloat16)
    keys = contract(w_key[...], normed, 0, 0).astype(jnp.bfloat16)
    values = contract(w_value[...], normed, 0, 0).astype(jnp.bfloat16)
    gates = jax.nn.sigmoid(contract(w_gate[...], normed, 0, 0))
    scale = HEAD_DIM ** (-0.5)
    for row in range(own_rows):
        span = slice(row * length, (row + 1) * length)
        for head in range(HEADS):
            part = slice(head * HEAD_DIM, (head + 1) * HEAD_DIM)
            scores = contract(keys[part, span], queries[part, span], 0, 0)
            expanded = jnp.exp((scores - jnp.max(scores, axis=0, keepdims=True)) * scale)
            total = jnp.sum(expanded, axis=0, keepdims=True)
            attended = contract(values[part, span], expanded.astype(jnp.bfloat16), 1, 0)
            merged_ref[part, span] = (attended * (1.0 / total) * gates[part, span]).astype(
                jnp.bfloat16
            )
    update = contract(w_out[...], merged_ref[...], 1, 0)
    rowwise = normalize(widened + update, upright(norm_mid[...], pairs)).astype(jnp.bfloat16)
    slots = count * padded
    send_ref[...] = (
        contract(outgoing(slots, padded, own_rows, length), rowwise, 1, 1)
        .astype(jnp.bfloat16)
        .reshape(count, padded, channels)
    )
    pl.semaphore_wait(barrier, count - 1)

    @pl.loop(1, count)
    def _(offset):
        transfer(offset).start()

    land_ref[me] = send_ref[me]
    arrange = incoming(slots, padded, own_rows, length)

    @pl.loop(1, count)
    def _(offset):
        transfer(offset).wait()

    mirrored = contract(land_ref[...].reshape(slots, channels), arrange, 0, 0)
    sym_ref[...] = ((rowwise.astype(jnp.float32) + mirrored) * 0.5).astype(jnp.bfloat16)


def transition_kernel(sym_ref, norm_out, w_up, w_down, out_ref):
    own_rows, channels, length = out_ref.shape
    flat = sym_ref[...].astype(jnp.float32)
    normed = normalize(flat, upright(norm_out[...], own_rows * length)).astype(jnp.bfloat16)
    hidden = jnp.maximum(contract(w_up[...], normed, 0, 0), 0.0).astype(jnp.bfloat16)
    result = (flat + contract(w_down[...], hidden, 1, 0)).astype(jnp.bfloat16)
    for row in range(own_rows):
        out_ref[row] = result[:, row * length : (row + 1) * length]


def local(
    pair_map, norm_in, w_query, w_key, w_value, w_gate, w_out, norm_mid, norm_out, w_up, w_down
):
    cols = lax.axis_size("col")
    count = lax.axis_size("row") * cols
    tile_rows, tile_cols, channels = pair_map.shape
    own_rows = tile_rows // cols
    length = tile_cols * cols
    pairs = own_rows * length
    padded = (own_rows * own_rows + 15) // 16 * 16
    rows = pair_map
    if cols > 1:
        halves = pair_map.reshape(cols, own_rows, tile_cols, channels)
        rows = lax.all_to_all(halves, "col", split_axis=0, concat_axis=2, tiled=True)[0]
    whole = pl.BlockSpec(memory_space=pltpu.VMEM)
    symmetric = pl.pallas_call(
        functools.partial(attend_kernel, count, cols),
        out_shape=jax.ShapeDtypeStruct((channels, pairs), jnp.bfloat16),
        in_specs=[whole] * 8,
        out_specs=whole,
        scratch_shapes=[
            pltpu.VMEM((w_query.shape[1], pairs), jnp.bfloat16),
            pltpu.VMEM((count, padded, channels), jnp.bfloat16),
            pltpu.VMEM((count, padded, channels), jnp.bfloat16),
            pltpu.SemaphoreType.DMA((count,)),
            pltpu.SemaphoreType.DMA((count,)),
        ],
        compiler_params=pltpu.CompilerParams(collective_id=0, has_side_effects=True),
    )(
        rows.transpose(0, 2, 1),
        norm_in[None],
        w_query,
        w_key,
        w_value,
        w_gate,
        w_out.T,
        norm_mid[None],
    )
    finished = pl.pallas_call(
        transition_kernel,
        out_shape=jax.ShapeDtypeStruct((own_rows, channels, length), jnp.bfloat16),
        in_specs=[whole] * 4,
        out_specs=whole,
    )(symmetric, norm_out[None], w_up, w_down.T).transpose(0, 2, 1)
    if cols == 1:
        return finished
    returned = lax.all_to_all(
        finished.reshape(own_rows, cols, tile_cols, channels),
        "col",
        split_axis=1,
        concat_axis=0,
        tiled=True,
    )
    return returned.reshape(tile_rows, tile_cols, channels)


def solution(mesh):
    placed = (P(("grp", "row"), "col", None), P(), P(), P(), P(), P(), P(), P(), P(), P(), P())
    return jax.shard_map(
        local, mesh=mesh, in_specs=placed, out_specs=P(("grp", "row"), "col", None), check_vma=False
    )
```

time: 41.4 us -> 28.2 us (0.68)
  the two profiles are of different devices: /device:TPU:0 before, /device:TPU:9 now
where the time goes in v2:
time: 28.2 us; the launch traced here: 27.9 us
  Pallas kernels  25.3 us (90%)
  local copies, waits for them, and re-layouts  2.61 us (9%)
    pallas_call x1, Pallas kernels, local(): pl.pallas_call(functools.partial(attend_kernel, count, cols), out_shape=j...  22 us
    pallas_call x1, Pallas kernels, local(): pl.pallas_call(transition_kernel, out_shape=jax.ShapeDtypeStruct((own_row...  3.37 us
    unnamed x6, local copies, waits for them, and re-layouts  0.89 us
    broadcast_in_dim x1, local copies, waits for them, and re-layouts, local(): norm_mid[None]  0.59 us

profile of v2, /device:TPU:9, one launch (start us, length us, event | category | flops | bytes accessed | tf_op | source)
XLA Modules:
  0.0 27.9 jit_solution(18087300894467743053)
XLA Ops:
  0.0 0.0 copy-start
  0.0 0.7 %copy-done = f32[288]{0:T(512)S(1)} copy-done((f32[288]{0:T(512)S(1)}, f32[288]{0:T(512)}, u32[]{:S(2)}) %copy-start) | copy-done | bytes 1176
  0.7 0.0 copy-start.1
  0.7 0.6 %broadcast_in_dim.9.norm_in = f32[1,288]{1,0:T(1,128)} reshape(f32[288]{0:T(512)S(1)} %copy-done) | data formatting | bytes 2304 | tf_op jit(solution)/shard_map/broadcast_in_dim | solution.py:186
  1.2 0.1 copy-done.1
  1.4 0.0 copy-start.2
  1.4 0.6 %broadcast_in_dim.10.norm_mid = f32[1,288]{1,0:T(1,128)} reshape(f32[288]{0:T(512)S(1)} %copy-done.1) | data formatting | bytes 2304 | tf_op jit(solution)/shard_map/broadcast_in_dim | solution.py:192
  2.0 0.1 copy-done.2
  2.0 0.6 %broadcast_in_dim.11.norm_out = f32[1,288]{1,0:T(1,128)} reshape(f32[288]{0:T(512)S(1)} %copy-done.2) | data formatting | bytes 2304 | tf_op jit(solution)/shard_map/broadcast_in_dim | solution.py:199
  2.6 22.0 %shard_map.109.sym_ref = bf16[288,512]{1,0:T(8,128)(2,1)} custom-call(bf16[4,288,128]{2,1,0:T(8,128)(2,1)} %bitcast.5, f32[1,288]{1,0:T(1,128)} %broadcast_in_dim.9.norm_in, bf16[288,256]{1,0:T(8,128)(2,1)} %w_query.1, bf16[288,256]{1,0:T(8,128)(2,1)} %w_key.1, bf16[288,256]{1,0:T(8,128)(2,1)} %w_value.1, bf16[288,256]{1,0:T(8,128)(2,1)} %w_gate.1, ...), custom_call_target="tpu_custom_call" | custom-call | tf_op jit(solution)/shard_map/pallas_call | solution.py:171
  24.6 3.4 %shard_map.110 = bf16[4,288,128]{2,1,0:T(8,128)(2,1)} custom-call(bf16[288,512]{1,0:T(8,128)(2,1)} %shard_map.109.sym_ref, f32[1,288]{1,0:T(1,128)} %broadcast_in_dim.11.norm_out, bf16[288,1152]{1,0:T(8,128)(2,1)} %w_up.1, bf16[288,1152]{1,0:T(8,128)(2,1)} %bitcast.4), custom_call_target="tpu_custom_call" | custom-call | tf_op jit(solution)/shard_map/pallas_call | solution.py:194
Async XLA Ops:
  0.0 0.7 %copy-start = (f32[288]{0:T(512)S(1)}, f32[288]{0:T(512)}, u32[]{:S(2)}) copy-start(f32[288]{0:T(512)} %param.12) | copy-start | bytes 3460
  0.7 0.7 %copy-start.1 = (f32[288]{0:T(512)S(1)}, f32[288]{0:T(512)}, u32[]{:S(2)}) copy-start(f32[288]{0:T(512)} %param.18) | copy-start | bytes 3460
  1.4 0.7 %copy-start.2 = (f32[288]{0:T(512)S(1)}, f32[288]{0:T(512)}, u32[]{:S(2)}) copy-start(f32[288]{0:T(512)} %param.19) | copy-start | bytes 3460

commit v3 on v2

v3 whole, which is shorter than its diff:
```python
import functools

import jax
import jax.numpy as jnp
from jax import lax
from jax.experimental import pallas as pl
from jax.experimental.pallas import tpu as pltpu
from jax.sharding import PartitionSpec as P

HEADS = 8
HEAD_DIM = 32
LANES = 128


epsilon = 1e-06


def normalize(inputs, gain):
    mean_square = jnp.mean(inputs * inputs, axis=0, keepdims=True)
    return inputs * lax.rsqrt(mean_square + epsilon) * gain


def contract(left, right, left_dim, right_dim):
    return lax.dot_general(
        left, right, (((left_dim,), (right_dim,)), ((), ())), preferred_element_type=jnp.float32
    )


def upright(gain, pairs):
    column = jnp.broadcast_to(gain[None], (LANES, gain.shape[0])).T
    return jnp.concatenate([column] * (pairs // LANES), axis=1)


def outgoing(slots, padded, phase_rows, own_rows, length):
    shape = (slots, phase_rows * length)
    slot = lax.broadcasted_iota(jnp.int32, shape, 0)
    pair = lax.broadcasted_iota(jnp.int32, shape, 1)
    within = slot % padded
    wanted = (within % phase_rows) * length + (slot // padded) * own_rows + within // phase_rows
    wanted = jnp.where(within < phase_rows * own_rows, wanted, -1)
    return jnp.where(pair == wanted, 1.0, 0.0).astype(jnp.bfloat16)


def incoming(phase, slots, padded, phase_rows, own_rows, length):
    shape = (slots, own_rows * length)
    slot = lax.broadcasted_iota(jnp.int32, shape, 0)
    pair = lax.broadcasted_iota(jnp.int32, shape, 1)
    device = (pair % length) // own_rows
    row = pair % own_rows
    wanted = device * padded + (pair // length) * phase_rows + row % phase_rows
    wanted = jnp.where(row // phase_rows == phase, wanted, -1)
    return jnp.where(slot == wanted, 1.0, 0.0).astype(jnp.bfloat16)


def attend_kernel(
    count,
    cols,
    x_ref,
    norm_in,
    w_query,
    w_key,
    w_value,
    w_gate,
    w_out,
    norm_mid,
    sym_ref,
    merged_ref,
    send_ref,
    land_ref,
    send_sem,
    recv_sem,
):
    own_rows, channels, length = x_ref.shape
    phases, _, padded, _ = send_ref.shape
    phase_rows = own_rows // phases
    phase_pairs = phase_rows * length
    slots = count * padded
    me = lax.axis_index("row") * cols + lax.axis_index("col")

    def place(offset):
        other = lax.rem(me + offset, count)
        return {"row": other // cols, "col": lax.rem(other, cols)}

    def transfer(phase, offset):
        other = lax.rem(me + offset, count)
        return pltpu.make_async_remote_copy(
            src_ref=send_ref.at[phase, other],
            dst_ref=land_ref.at[phase, me],
            send_sem=send_sem.at[phase, offset],
            recv_sem=recv_sem.at[phase, offset],
            device_id=place(offset),
            device_id_type=pl.DeviceIdType.MESH,
        )

    barrier = pltpu.get_barrier_semaphore()

    @pl.loop(1, count)
    def _(offset):
        pl.semaphore_signal(
            barrier, inc=1, device_id=place(offset), device_id_type=pl.DeviceIdType.MESH
        )

    gain_in = upright(norm_in[...], phase_pairs)
    gain_mid = upright(norm_mid[...], phase_pairs)
    ordering = outgoing(slots, padded, phase_rows, own_rows, length)
    scale = HEAD_DIM ** (-0.5)
    finished = []
    for phase in range(phases):
        rows = range(phase * phase_rows, (phase + 1) * phase_rows)
        widened = jnp.concatenate([x_ref[row] for row in rows], axis=1).astype(jnp.float32)
        normed = normalize(widened, gain_in).astype(jnp.bfloat16)
        queries = contract(w_query[...], normed, 0, 0).astype(jnp.bfloat16)
        keys = contract(w_key[...], normed, 0, 0).astype(jnp.bfloat16)
        values = contract(w_value[...], normed, 0, 0).astype(jnp.bfloat16)
        gates = jax.nn.sigmoid(contract(w_gate[...], normed, 0, 0))
        for row in range(phase_rows):
            span = slice(row * length, (row + 1) * length)
            for head in range(HEADS):
                part = slice(head * HEAD_DIM, (head + 1) * HEAD_DIM)
                scores = contract(keys[part, span], queries[part, span], 0, 0)
                expanded = jnp.exp((scores - jnp.max(scores, axis=0, keepdims=True)) * scale)
                total = jnp.sum(expanded, axis=0, keepdims=True)
                attended = contract(values[part, span], expanded.astype(jnp.bfloat16), 1, 0)
                merged_ref[phase, part, span] = (
                    attended * (1.0 / total) * gates[part, span]
                ).astype(jnp.bfloat16)
        update = contract(w_out[...], merged_ref[phase], 1, 0)
        rowwise = normalize(widened + update, gain_mid).astype(jnp.bfloat16)
        finished.append(rowwise)
        send_ref[phase] = (
            contract(ordering, rowwise, 1, 1)
            .reshape(count, padded, channels)
            .astype(jnp.bfloat16)
        )
        if phase == 0:
            pl.semaphore_wait(barrier, count - 1)

        @pl.loop(1, count)
        def _(offset, phase=phase):
            transfer(phase, offset).start()

        land_ref[phase, me] = send_ref[phase, me]

    total = jnp.concatenate(finished, axis=1).astype(jnp.float32)
    for phase in range(phases):
        arrange = incoming(phase, slots, padded, phase_rows, own_rows, length)

        @pl.loop(1, count)
        def _(offset, phase=phase):
            transfer(phase, offset).wait()

        landed = land_ref[phase].astype(jnp.float32).reshape(slots, channels)
        total += contract(landed.astype(jnp.bfloat16), arrange, 0, 0)
    sym_ref[...] = (total * 0.5).astype(jnp.bfloat16)


def transition_kernel(sym_ref, norm_out, w_up, w_down, out_ref):
    own_rows, channels, length = out_ref.shape
    flat = sym_ref[...].astype(jnp.float32)
    normed = normalize(flat, upright(norm_out[...], own_rows * length)).astype(jnp.bfloat16)
    hidden = jnp.maximum(contract(w_up[...], normed, 0, 0), 0.0).astype(jnp.bfloat16)
    result = (flat + contract(w_down[...], hidden, 1, 0)).astype(jnp.bfloat16)
    for row in range(own_rows):
        out_ref[row] = result[:, row * length : (row + 1) * length]


def local(
    pair_map, norm_in, w_query, w_key, w_value, w_gate, w_out, norm_mid, norm_out, w_up, w_down
):
    cols = lax.axis_size("col")
    count = lax.axis_size("row") * cols
    tile_rows, tile_cols, channels = pair_map.shape
    own_rows = tile_rows // cols
    length = tile_cols * cols
    pairs = own_rows * length
    phases = 2 if own_rows % 2 == 0 else 1
    padded = (own_rows // phases * own_rows + 7) // 8 * 8
    rows = pair_map
    if cols > 1:
        halves = pair_map.reshape(cols, own_rows, tile_cols, channels)
        rows = lax.all_to_all(halves, "col", split_axis=0, concat_axis=2, tiled=True)[0]
    whole = pl.BlockSpec(memory_space=pltpu.VMEM)
    symmetric = pl.pallas_call(
        functools.partial(attend_kernel, count, cols),
        out_shape=jax.ShapeDtypeStruct((channels, pairs), jnp.bfloat16),
        in_specs=[whole] * 8,
        out_specs=whole,
        scratch_shapes=[
            pltpu.VMEM((phases, w_query.shape[1], pairs // phases), jnp.bfloat16),
            pltpu.VMEM((phases, count, padded, channels), jnp.bfloat16),
            pltpu.VMEM((phases, count, padded, channels), jnp.bfloat16),
            pltpu.SemaphoreType.DMA((phases, count)),
            pltpu.SemaphoreType.DMA((phases, count)),
        ],
        compiler_params=pltpu.CompilerParams(collective_id=0, has_side_effects=True),
    )(
        rows.transpose(0, 2, 1),
        norm_in,
        w_query,
        w_key,
        w_value,
        w_gate,
        w_out.T,
        norm_mid,
    )
    finished = pl.pallas_call(
        transition_kernel,
        out_shape=jax.ShapeDtypeStruct((own_rows, channels, length), jnp.bfloat16),
        in_specs=[whole] * 4,
        out_specs=whole,
    )(symmetric, norm_out, w_up, w_down.T).transpose(0, 2, 1)
    if cols == 1:
        return finished
    returned = lax.all_to_all(
        finished.reshape(own_rows, cols, tile_cols, channels),
        "col",
        split_axis=1,
        concat_axis=0,
        tiled=True,
    )
    return returned.reshape(tile_rows, tile_cols, channels)


def solution(mesh):
    placed = (P(("grp", "row"), "col", None), P(), P(), P(), P(), P(), P(), P(), P(), P(), P())
    return jax.shard_map(
        local, mesh=mesh, in_specs=placed, out_specs=P(("grp", "row"), "col", None), check_vma=False
    )
```

time: 28.2 us -> 23.9 us (0.85)
  the two profiles are of different devices: /device:TPU:9 before, /device:TPU:0 now
where the time goes in v3:
time: 23.9 us; the launch traced here: 23.7 us
  Pallas kernels  23.7 us (99%)
    pallas_call x1, Pallas kernels, local(): pl.pallas_call(functools.partial(attend_kernel, count, cols), out_shape=j...  20.3 us
    pallas_call x1, Pallas kernels, local(): pl.pallas_call(transition_kernel, out_shape=jax.ShapeDtypeStruct((own_row...  3.37 us

profile of v3, /device:TPU:0, one launch (start us, length us, event | category | flops | bytes accessed | tf_op | source)
XLA Modules:
  0.0 23.7 jit_solution(15963195242601240871)
XLA Ops:
  0.0 20.3 %shard_map.109.sym_ref = bf16[288,512]{1,0:T(8,128)(2,1)} custom-call(bf16[4,288,128]{2,1,0:T(8,128)(2,1)} %bitcast.5, f32[288]{0:T(512)} %norm_in.1, bf16[288,256]{1,0:T(8,128)(2,1)} %w_query.1, bf16[288,256]{1,0:T(8,128)(2,1)} %w_key.1, bf16[288,256]{1,0:T(8,128)(2,1)} %w_value.1, bf16[288,256]{1,0:T(8,128)(2,1)} %w_gate.1, bf16[288,256]{1,0:T(8,128)(2,1)} %bitcast.6, ...), custom_call_target="tpu_custom_call" | custom-call | tf_op jit(solution)/shard_map/pallas_call | solution.py:183
  20.4 3.4 %shard_map.110 = bf16[4,288,128]{2,1,0:T(8,128)(2,1)} custom-call(bf16[288,512]{1,0:T(8,128)(2,1)} %shard_map.109.sym_ref, f32[288]{0:T(512)} %norm_out.1, bf16[288,1152]{1,0:T(8,128)(2,1)} %w_up.1, bf16[288,1152]{1,0:T(8,128)(2,1)} %bitcast.4), custom_call_target="tpu_custom_call" | custom-call | tf_op jit(solution)/shard_map/pallas_call | solution.py:206

commit v4 on v3

--- a/solution.py
+++ b/solution.py
@@ -137,7 +137,7 @@
 
         @pl.loop(1, count)
         def _(offset, phase=phase):
-            transfer(phase, offset).start()
+            transfer(phase, 1 + lax.rem(offset + count // 2, count - 1)).start()
 
         land_ref[phase, me] = send_ref[phase, me]
 

time: 23.9 us -> 25 us (1.046)
  Pallas kernels: 23.7 us -> 24.9 us
    pallas_call x1, Pallas kernels: 20.3 us -> 21.5 us  [local(): pl.pallas_call(functools.partial(attend_kernel, count, cols), out_shape=j...]
where the time goes in v4:
time: 25 us; the launch traced here: 24.9 us
  Pallas kernels  24.9 us (100%)
    pallas_call x1, Pallas kernels, local(): pl.pallas_call(functools.partial(attend_kernel, count, cols), out_shape=j...  21.5 us
    pallas_call x1, Pallas kernels, local(): pl.pallas_call(transition_kernel, out_shape=jax.ShapeDtypeStruct((own_row...  3.37 us

profile of v4, /device:TPU:0, one launch (start us, length us, event | category | flops | bytes accessed | tf_op | source)
XLA Modules:
  0.0 24.9 jit_solution(18115205533702822700)
XLA Ops:
  0.0 21.5 %shard_map.109.sym_ref = bf16[288,512]{1,0:T(8,128)(2,1)} custom-call(bf16[4,288,128]{2,1,0:T(8,128)(2,1)} %bitcast.5, f32[288]{0:T(512)} %norm_in.1, bf16[288,256]{1,0:T(8,128)(2,1)} %w_query.1, bf16[288,256]{1,0:T(8,128)(2,1)} %w_key.1, bf16[288,256]{1,0:T(8,128)(2,1)} %w_value.1, bf16[288,256]{1,0:T(8,128)(2,1)} %w_gate.1, bf16[288,256]{1,0:T(8,128)(2,1)} %bitcast.6, ...), custom_call_target="tpu_custom_call" | custom-call | tf_op jit(solution)/shard_map/pallas_call | solution.py:183
  21.5 3.4 %shard_map.110 = bf16[4,288,128]{2,1,0:T(8,128)(2,1)} custom-call(bf16[288,512]{1,0:T(8,128)(2,1)} %shard_map.109.sym_ref, f32[288]{0:T(512)} %norm_out.1, bf16[288,1152]{1,0:T(8,128)(2,1)} %w_up.1, bf16[288,1152]{1,0:T(8,128)(2,1)} %bitcast.4), custom_call_target="tpu_custom_call" | custom-call | tf_op jit(solution)/shard_map/pallas_call | solution.py:206
